TPU v7x, 512 devices: a whole 4x8x8 slice. The times are simulated.
512 devices in a mesh: space: 128 (over x, y, z_hi, core), modes: 4 (over z_lo).
Axes of the slice: x: 4, y: 8, z: 8 (z_hi: 2, z_lo: 4; z = z_hi * 4 + z_lo), core: 2. Of those that a mesh axis runs over, the one named last changes fastest.
Arguments:
- voltage_expansion: float32 [220, 128, 2048], P('modes', 'space'), may hold values from -6 to 6
- current_injection: float32 [220, 128, 2048], P('modes', 'space'), may hold values from -48 to 48
- thermal_state: float32 [220, 128, 2048], P('modes', 'space'), may hold values from -6 to 6
- average_electric_transport: float32 [128, 2048], P('space'), may hold values from 0.5 to 4
- material_zone: int32 [128, 2048], P('space'), may hold values from 0 to 3
- zone_relative_response: float32 [4, 9], replicated, may hold values from 0.02 to 0.12
- polynomial_exponent_rows: int32 [220, 9], replicated, may hold values from 0 to 3, as said below
- quadrature_abscissa_choice: int32 [512, 9], replicated, may hold values from 0 to 4
- quadrature_integer_share: int32 [512], replicated, may hold values from 1 to 1024
Outputs:
- relaxed_voltage: float32 [220, 128, 2048], P('modes', 'space')
- advanced_thermal_state: float32 [220, 128, 2048], P('modes', 'space')
Inputs may be any that keep to these rules, and one draw needn't show every extreme that they name: `polynomial_exponent_rows`: the rows are the 220 multi-indices of total degree at most 3 over 9 parameters, each once.
All inputs are finite; a program needn't handle non-finite values.
Results may differ from a plain program's by a relative error of at most 0.0003.
Values sent between devices are 32-bit elements; how exact they have to be, the bound alone decides.
A program may use at most 64 MiB of HBM per device.

v0:
```python
import jax
import jax.numpy as jnp
from jax import lax
from jax.sharding import PartitionSpec as P

NY = 256
NZ = 8
HERMITE_NODES = (
    0.0,
    1.355626179974266,
    -1.355626179974266,
    2.8569700138728056,
    -2.8569700138728056,
)


def padded_2(block, sides, width):
    for axis, dim in sides:
        count = lax.axis_size(axis)
        forward = [(i, i + 1) for i in range(count - 1)]
        backward = [(target, source) for source, target in forward]
        low = lax.ppermute(
            lax.slice_in_dim(block, block.shape[dim] - width, None, axis=dim), axis, forward
        )
        high = lax.ppermute(lax.slice_in_dim(block, 0, width, axis=dim), axis, backward)
        block = jnp.concatenate([low, block, high], axis=dim)
    return block


def neighbours(field):
    column_ids = jnp.arange(field.shape[-1])
    depth_pos = column_ids % NZ
    row_pos = column_ids // NZ
    z_next = jnp.where(depth_pos < NZ - 1, jnp.roll(field, -1, -1), 0.0)
    z_prev = jnp.where(depth_pos > 0, jnp.roll(field, 1, -1), 0.0)
    y_next = jnp.where(row_pos < NY - 1, jnp.roll(field, -NZ, -1), 0.0)
    y_prev = jnp.where(row_pos > 0, jnp.roll(field, NZ, -1), 0.0)
    return (z_next, z_prev, y_next, y_prev)


def diffusion_operator_weights(padded):
    center = padded[..., 1:-1, :]
    z_next, z_prev, y_next, y_prev = neighbours(center)
    return (
        6.0 * center - padded[..., 2:, :] - padded[..., :-2, :] - z_next - z_prev - y_next - y_prev
    )


def gradient(padded):
    center = padded[..., 1:-1, :]
    z_next, z_prev, y_next, y_prev = neighbours(center)
    along_x = (padded[..., 2:, :] - padded[..., :-2, :]) * 0.5
    along_y = (y_next - y_prev) * 0.5
    along_z = (z_next - z_prev) * 0.5
    return jnp.stack([along_x, along_y, along_z])


def coupling(row_table, col_table):
    offsets = row_table[:, None, :] - col_table[None, :, :]
    differ_count = jnp.sum((offsets != 0).astype(jnp.int32), axis=2)
    layers = [jnp.where(differ_count == 0, 1.0, 0.0).astype(jnp.float32)]
    for which_param in range(row_table.shape[1]):
        larger = jnp.maximum(
            row_table[:, None, which_param], col_table[None, :, which_param]
        ).astype(jnp.float32)
        linked = (jnp.abs(offsets[:, :, which_param]) == 1) & (differ_count == 1)
        layers.append(jnp.where(linked, jnp.sqrt(larger), 0.0))
    return jnp.stack(layers)


def node_values(quadrature_abscissa_choice):
    node_vals = jnp.zeros(quadrature_abscissa_choice.shape, jnp.float32)
    for which_node in range(5):
        node_vals = node_vals + jnp.where(
            quadrature_abscissa_choice == which_node, HERMITE_NODES[which_node], 0.0
        )
    return node_vals


def basis_values(polynomial_exponent_rows, node_vals):
    poly_terms = [
        jnp.ones_like(node_vals),
        node_vals,
        (node_vals * node_vals - 1.0) / jnp.sqrt(2.0),
        (node_vals * node_vals * node_vals - 3.0 * node_vals) / jnp.sqrt(6.0),
    ]
    basis_vals = jnp.ones((node_vals.shape[0], polynomial_exponent_rows.shape[0]), jnp.float32)
    for which_param in range(polynomial_exponent_rows.shape[1]):
        degree = polynomial_exponent_rows[:, which_param]
        factor = jnp.zeros_like(basis_vals)
        for which_deg in range(4):
            factor = factor + jnp.where(
                degree[None, :] == which_deg, poly_terms[which_deg][:, which_param][:, None], 0.0
            )
        basis_vals = basis_vals * factor
    return basis_vals


def on_device(
    voltage_expansion,
    current_injection,
    thermal_state,
    average_electric_transport,
    material_zone,
    zone_relative_response,
    polynomial_exponent_rows,
    quadrature_abscissa_choice,
    quadrature_integer_share,
):
    hp = lax.Precision.HIGHEST
    modes_here = voltage_expansion.shape[0]
    planes = voltage_expansion.shape[1]
    columns = voltage_expansion.shape[2]
    cell_count = planes * columns
    nreg = zone_relative_response.shape[0]
    all_modes = polynomial_exponent_rows.shape[0]
    num_points = quadrature_integer_share.shape[0]
    first_mode = lax.axis_index("modes") * modes_here
    own_table = lax.dynamic_slice_in_dim(polynomial_exponent_rows, first_mode, modes_here, 0)
    bordered_quantities = padded_2(
        jnp.stack([voltage_expansion, thermal_state]), (("space", 2),), 1
    )
    pot_padded = bordered_quantities[0]
    thermal_state_bordered = bordered_quantities[1]
    sens_cell = jnp.zeros((zone_relative_response.shape[1],) + material_zone.shape, jnp.float32)
    for which_region in range(nreg):
        sens_cell = sens_cell + jnp.where(
            material_zone[None] == which_region,
            zone_relative_response[which_region][:, None, None],
            0.0,
        )
    coeff = (
        jnp.concatenate([jnp.ones((1,) + material_zone.shape, jnp.float32), sens_cell])
        * average_electric_transport
    )
    coeff_flat = coeff.reshape(coeff.shape[0], cell_count)
    flat_rough = diffusion_operator_weights(pot_padded).reshape(modes_here, cell_count)
    row_coup = coupling(own_table, polynomial_exponent_rows)
    mixed = jnp.einsum(
        "mij,jc->mic",
        row_coup,
        lax.all_gather(flat_rough, "modes", axis=0, tiled=True),
        precision=hp,
    )
    applied = jnp.sum(coeff_flat[:, None, :] * mixed, axis=0)
    applied = applied.reshape(modes_here, planes, columns)
    relaxed_voltage = voltage_expansion + 0.8 * (current_injection - applied) / (
        6.0 * average_electric_transport
    )
    node_vals = node_values(quadrature_abscissa_choice)
    basis_vals = basis_values(polynomial_exponent_rows, node_vals)
    new_padded = padded_2(relaxed_voltage, (("space", 1),), 1)
    grads = gradient(new_padded)
    point_grads = jnp.einsum(
        "qi,kixn->kqxn",
        basis_vals,
        lax.all_to_all(grads, "modes", split_axis=3, concat_axis=1, tiled=True),
        precision=hp,
    )
    quarter = columns // lax.axis_size("modes")
    offset = lax.axis_index("modes") * quarter
    cond_part = lax.dynamic_slice_in_dim(average_electric_transport, offset, quarter, 1)
    region_part = lax.dynamic_slice_in_dim(material_zone, offset, quarter, 1)
    cond_lift = 1.0 + jnp.dot(zone_relative_response, node_vals.T, precision=hp)
    spread = jnp.zeros((num_points, planes, quarter), jnp.float32)
    for which_region in range(nreg):
        spread = spread + jnp.where(
            region_part[None] == which_region, cond_lift[which_region][:, None, None], 0.0
        )
    joule_heat = cond_part * spread * jnp.sum(point_grads * point_grads, axis=0)
    weighted = (
        basis_vals.T
        * quadrature_integer_share[None, :].astype(jnp.float32)
        / (512.0 * num_points * all_modes)
    )
    heat_points = jnp.einsum("iq,qxn->ixn", weighted, joule_heat, precision=hp)
    thermal_expansion_terms = lax.all_to_all(
        heat_points, "modes", split_axis=0, concat_axis=2, tiled=True
    )
    advanced_thermal_state = thermal_state + 0.1 * (
        thermal_expansion_terms - 1.5 * diffusion_operator_weights(thermal_state_bordered)
    )
    return (relaxed_voltage, advanced_thermal_state)


def solution(mesh):
    in_specs = (
        P("modes", "space", None),
        P("modes", "space", None),
        P("modes", "space", None),
        P("space", None),
        P("space", None),
        P(),
        P(),
        P(),
        P(),
    )
    out_specs = (P("modes", "space", None), P("modes", "space", None))
    return jax.shard_map(
        on_device, mesh=mesh, in_specs=in_specs, out_specs=out_specs, check_vma=False
    )
```

profile of v0, /device:TPU:59, one launch (start us, length us, event | category | flops | bytes accessed | tf_op | source)
XLA Modules:
  0.0 265.5 jit_solution(5457627602112726379)
XLA Ops:
  9.5 2.6 collective-permute-start.1
  12.1 10.5 %collective-permute-start = (f32[2,55,1,2048]{3,0,2,1:T(2,128)S(1)}, f32[2,55,1,2048]{3,0,2,1:T(2,128)}, u32[]{:S(2)}, u32[]{:S(2)}) collective-permute-start(f32[2,55,1,2048]{3,0,2,1:T(2,128)S(1)} %copy.62), channel_id=1, source_target_pairs={{0,4},{4,8},{8,12},{12,16},{16,20},{20,24},{24,28},{28,32},{32,36}... | collective-permute-start | bytes 2703368 | tf_op jit(solution)/shard_map/ppermute | solution.py:22
  27.4 27.7 %collective-permute-done.1 = f32[2,55,1,2048]{3,0,2,1:T(2,128)} collective-permute-done((f32[2,55,1,2048]{3,0,2,1:T(2,128)S(1)}, f32[2,55,1,2048]{3,0,2,1:T(2,128)}, u32[]{:S(2)}, u32[]{:S(2)}) %collective-permute-start.1) | collective-permute-done | bytes 901152 | tf_op jit(solution)/shard_map/ppermute | solution.py:25
  56.7 8.6 %collective-permute-done = f32[2,55,1,2048]{3,0,2,1:T(2,128)} collective-permute-done((f32[2,55,1,2048]{3,0,2,1:T(2,128)S(1)}, f32[2,55,1,2048]{3,0,2,1:T(2,128)}, u32[]{:S(2)}, u32[]{:S(2)}) %collective-permute-start) | collective-permute-done | bytes 901152 | tf_op jit(solution)/shard_map/ppermute | solution.py:22
  74.1 42.7 %all-gather.3.cloned.1.call-done = f32[220,1,2048]{2,1,0:T(1,128)} async-done(((f32[55,1,2048]{2,1,0:T(1,128)}), f32[220,1,2048]{2,1,0:T(1,128)}) %all-gather.3.cloned.1.call-update) | async-done | bytes 1802256 | tf_op jit(solution)/shard_map/all_gather | solution.py:142
  116.8 5.9 %multiply_reduce_fusion = f32[55,2048]{1,0:T(8,128)S(1)} fusion(f32[10,55,220]{2,1,0:T(8,128)} %select_dynamic-update-slice_fusion, f32[10,2048]{1,0:T(8,128)S(1)} %multiply_bitcast_fusion.1, f32[220,1,2048]{2,1,0:T(1,128)} %all-gather.3.cloned.1.call-done), kind=kOutput, calls=%fused_computation | convolution fusion | flops 2975836160 | bytes 2818720 | tf_op jit(solution)/shard_map/mij,jc->mic/dot_general | solution.py:139
  123.7 3.1 %collective-permute-start.2 = (f32[55,1,2048]{2,0,1:T(8,128)S(1)}, f32[55,1,2048]{2,0,1:T(8,128)S(1)}, u32[]{:S(2)}, u32[]{:S(2)}) collective-permute-start(f32[55,1,2048]{2,0,1:T(8,128)S(1)} %fusion.40), channel_id=1, source_target_pairs={{4,0},{8,4},{12,8},{16,12},{20,16},{24,20},{28,24},{32,28},{36,32}... | collective-permute-start | bytes 1351688 | tf_op jit(solution)/shard_map/ppermute | solution.py:25
  126.8 6.6 %collective-permute-start.3 = (f32[55,1,2048]{2,0,1:T(8,128)S(1)}, f32[55,1,2048]{2,0,1:T(8,128)S(1)}, u32[]{:S(2)}, u32[]{:S(2)}) collective-permute-start(f32[55,1,2048]{2,0,1:T(8,128)S(1)} %fusion.40), channel_id=1, source_target_pairs={{0,4},{4,8},{8,12},{12,16},{16,20},{20,24},{24,28},{28,32},{32,36}... | collective-permute-start | bytes 1351688 | tf_op jit(solution)/shard_map/ppermute | solution.py:22
  133.7 9.7 %collective-permute-done.2 = f32[55,1,2048]{2,0,1:T(8,128)S(1)} collective-permute-done((f32[55,1,2048]{2,0,1:T(8,128)S(1)}, f32[55,1,2048]{2,0,1:T(8,128)S(1)}, u32[]{:S(2)}, u32[]{:S(2)}) %collective-permute-start.2) | collective-permute-done | bytes 450592 | tf_op jit(solution)/shard_map/ppermute | solution.py:25
  143.4 11.2 %collective-permute-done.3 = f32[55,1,2048]{2,0,1:T(8,128)S(1)} collective-permute-done((f32[55,1,2048]{2,0,1:T(8,128)S(1)}, f32[55,1,2048]{2,0,1:T(8,128)S(1)}, u32[]{:S(2)}, u32[]{:S(2)}) %collective-permute-start.3) | collective-permute-done | bytes 450592 | tf_op jit(solution)/shard_map/ppermute | solution.py:22
  154.8 3.1 %copy.71 = f32[3,55,1,2048]{1,0,2,3:T(4,128)} copy(f32[3,55,1,2048]{3,1,2,0:T(8,128)S(1)} %pad_maximum_fusion.1) | data formatting | bytes 2703360 | tf_op jit(solution)/shard_map/stack | solution.py:55
  157.9 6.6 %reshape.2106 = f32[4,1,84480]{2,1,0:T(1,128)} reshape(f32[2048,1,3,55]{3,2,1,0:T(4,128)} %bitcast.196) | data formatting | bytes 2703360
  164.6 3.7 %all-to-all-start = ((f32[4,1,84480]{2,1,0:T(1,128)}), f32[4,1,84480]{2,1,0:T(1,128)S(1)}, u32[]{:S(2)}, u32[]{:S(2)}) async-start(f32[4,1,84480]{2,1,0:T(1,128)} %reshape.2106), calls=%async_computation | async-start | bytes 2703360 | tf_op jit(solution)/shard_map/all_to_all | solution.py:157
  169.7 29.8 %all-to-all-done = f32[4,1,84480]{2,1,0:T(1,128)S(1)} async-done(((f32[4,1,84480]{2,1,0:T(1,128)}), f32[4,1,84480]{2,1,0:T(1,128)S(1)}, u32[]{:S(2)}, u32[]{:S(2)}) %all-to-all-start) | async-done | bytes 1351712 | tf_op jit(solution)/shard_map/all_to_all | solution.py:157
  200.1 5.6 %reduce.20 = f32[4,84480]{1,0:T(4,128)} reduce(f32[4,1,84480]{2,1,0:T(1,128)S(1)} %all-to-all-done, f32[]{:T(128)} %broadcast.1558), dimensions={1}, to_apply=%all_to_all.24.reduce_sub_computation | reduce | bytes 2703364 | tf_op jit(solution)/shard_map/all_to_all | solution.py:157
  205.7 6.9 %reshape.2107 = f32[2048,1,3,55]{3,2,1,0:T(4,128)} reshape(f32[4,84480]{1,0:T(4,128)} %reduce.20) | data formatting | bytes 2703360
  212.6 4.6 %copy.79 = f32[3,55,1,4,512]{4,3,1,0,2:T(4,128)} copy(f32[3,55,1,4,512]{1,0,4,3,2:T(4,128)} %bitcast.197) | data formatting | bytes 2703360 | tf_op jit(solution)/shard_map/all_to_all | solution.py:157
  220.3 6.3 %multiply_reduce_fusion.1 = f32[512,512]{1,0:T(8,128)S(1)} fusion(f32[3,220,512]{2,1,0:T(8,128)} %reshape.2092, f32[512]{0:T(512)S(1)} %bitcast.231, f32[512]{0:T(512)S(1)} %bitcast.279, f32[512]{0:T(512)S(1)} %bitcast.259, f32[220]{0:T(256)S(1)} %get-tuple-element.133, f32[512]{0:T(512)S(1)} %bitcast.233, f32[512]{0:T(512)S(1)} %bitcast.277, ...), kind=kOutput, calls=%fused_computation.1 | convolution fusion | flops 2084474880 | bytes 2469412 | tf_op jit(solution)/shard_map/qi,kixn->kqxn/dot_general | solution.py:154
  226.6 3.1 %convolution_bitcast_fusion = f32[220,1,512]{2,0,1:T(8,128)S(1)} fusion(f32[512,512]{1,0:T(8,128)S(1)} %multiply_reduce_fusion.1, f32[512]{0:T(512)S(1)} %bitcast.285, f32[512]{0:T(512)S(1)} %bitcast.286, f32[512]{0:T(512)S(1)} %bitcast.287, f32[512]{0:T(512)S(1)} %bitcast.284, f32[512]{0:T(512)S(1)} %bitcast.283, pred[512]{0:T(512)(128)(4,1)S(1)} %copy-done.13, ...), kind=kOutput, calls=%fused_computation.8 | convolution fusion | flops 701628416 | bytes 1582628 | tf_op jit(solution)/shard_map/iq,qxn->ixn/dot_general | solution.py:176
  230.9 3.7 %all-to-all-start.1 = ((f32[220,1,512]{2,1,0:T(1,128)}), f32[220,1,512]{2,1,0:T(1,128)S(1)}, u32[]{:S(2)}, u32[]{:S(2)}) async-start(f32[220,1,512]{2,1,0:T(1,128)} %copy.74), calls=%async_computation.1 | async-start | bytes 901120 | tf_op jit(solution)/shard_map/all_to_all | solution.py:177
  236.2 11.5 %all-to-all-done.1 = f32[220,1,512]{2,1,0:T(1,128)S(1)} async-done(((f32[220,1,512]{2,1,0:T(1,128)}), f32[220,1,512]{2,1,0:T(1,128)S(1)}, u32[]{:S(2)}, u32[]{:S(2)}) %all-to-all-start.1) | async-done | bytes 450592 | tf_op jit(solution)/shard_map/all_to_all | solution.py:177
  249.6 1.9 all_to_all.28
  251.6 2.1 copy.75
  253.6 2.1 all_to_all.30
  (109 shorter events, 31.3 us)
Async XLA Ops:
  7.2 109.7 %all-gather.3.cloned.1.call-start = ((), (), s32[]{:S(2)}) async-start(), calls=%async_computation.2 | async-start | bytes 2252800 | tf_op jit(solution)/shard_map/all_gather | solution.py:142
  8.7 14.0 %copy-start.4 = (s32[220,9]{0,1:T(8,128)S(1)}, s32[220,9]{0,1:T(8,128)}, u32[]{:S(2)}) copy-start(s32[220,9]{0,1:T(8,128)} %param.15) | copy-start | bytes 23764
  8.7 14.9 %copy-start.7 = (s32[1,2048]{1,0:T(1,128)S(1)}, s32[1,2048]{1,0:T(1,128)}, u32[]{:S(2)}) copy-start(s32[1,2048]{1,0:T(1,128)} %param.13) | copy-start | bytes 24580
  8.8 15.6 %copy-start.5 = (f32[1,2048]{1,0:T(1,128)S(1)}, f32[1,2048]{1,0:T(1,128)}, u32[]{:S(2)}) copy-start(f32[1,2048]{1,0:T(1,128)} %param.12) | copy-start | bytes 24580
  8.8 15.6 %copy-start.8 = (s32[512]{0:T(512)S(1)}, s32[512]{0:T(512)}, u32[]{:S(2)}) copy-start(s32[512]{0:T(512)} %param.17) | copy-start | bytes 6148
  8.8 16.4 %copy-start.9 = (f32[4,9]{1,0:T(4,128)S(1)}, f32[4,9]{1,0:T(4,128)}, u32[]{:S(2)}) copy-start(f32[4,9]{1,0:T(4,128)} %param.14) | copy-start | bytes 436
  9.5 45.6 %collective-permute-start.1 = (f32[2,55,1,2048]{3,0,2,1:T(2,128)S(1)}, f32[2,55,1,2048]{3,0,2,1:T(2,128)}, u32[]{:S(2)}, u32[]{:S(2)}) collective-permute-start(f32[2,55,1,2048]{3,0,2,1:T(2,128)S(1)} %copy.62), channel_id=1, source_target_pairs={{4,0},{8,4},{12,8},{16,12},{20,16},{24,20},{28,24},{32,28},{36,32}... | collective-permute-start | bytes 2703368 | tf_op jit(solution)/shard_map/ppermute | solution.py:25
  12.1 53.3 %collective-permute-start = (f32[2,55,1,2048]{3,0,2,1:T(2,128)S(1)}, f32[2,55,1,2048]{3,0,2,1:T(2,128)}, u32[]{:S(2)}, u32[]{:S(2)}) collective-permute-start(f32[2,55,1,2048]{3,0,2,1:T(2,128)S(1)} %copy.62), channel_id=1, source_target_pairs={{0,4},{4,8},{8,12},{12,16},{16,20},{20,24},{24,28},{28,32},{32,36}... | collective-permute-start | bytes 2703368 | tf_op jit(solution)/shard_map/ppermute | solution.py:22
  74.1 48.7 %copy-start.2 = (f32[55,1,2048]{2,1,0:T(1,128)S(1)}, f32[55,1,2048]{2,1,0:T(1,128)}, u32[]{:S(2)}) copy-start(f32[55,1,2048]{2,1,0:T(1,128)} %param.9) | copy-start | bytes 1351684
  74.1 48.7 %copy-start.3 = (f32[55,1,2048]{2,1,0:T(1,128)S(1)}, f32[55,1,2048]{2,1,0:T(1,128)}, u32[]{:S(2)}) copy-start(f32[55,1,2048]{2,1,0:T(1,128)} %param.10) | copy-start | bytes 1351684
  123.7 19.7 %collective-permute-start.2 = (f32[55,1,2048]{2,0,1:T(8,128)S(1)}, f32[55,1,2048]{2,0,1:T(8,128)S(1)}, u32[]{:S(2)}, u32[]{:S(2)}) collective-permute-start(f32[55,1,2048]{2,0,1:T(8,128)S(1)} %fusion.40), channel_id=1, source_target_pairs={{4,0},{8,4},{12,8},{16,12},{20,16},{24,20},{28,24},{32,28},{36,32}... | collective-permute-start | bytes 1351688 | tf_op jit(solution)/shard_map/ppermute | solution.py:25
  126.8 27.9 %collective-permute-start.3 = (f32[55,1,2048]{2,0,1:T(8,128)S(1)}, f32[55,1,2048]{2,0,1:T(8,128)S(1)}, u32[]{:S(2)}, u32[]{:S(2)}) collective-permute-start(f32[55,1,2048]{2,0,1:T(8,128)S(1)} %fusion.40), channel_id=1, source_target_pairs={{0,4},{4,8},{8,12},{12,16},{16,20},{20,24},{24,28},{28,32},{32,36}... | collective-permute-start | bytes 1351688 | tf_op jit(solution)/shard_map/ppermute | solution.py:22
  164.6 3.7 %copy-start.6 = (s32[512,9]{0,1:T(8,128)S(1)}, s32[512,9]{0,1:T(8,128)}, u32[]{:S(2)}) copy-start(s32[512,9]{0,1:T(8,128)} %param.16) | copy-start | bytes 55300
  164.6 35.0 %all-to-all-start = ((f32[4,1,84480]{2,1,0:T(1,128)}), f32[4,1,84480]{2,1,0:T(1,128)S(1)}, u32[]{:S(2)}, u32[]{:S(2)}) async-start(f32[4,1,84480]{2,1,0:T(1,128)} %reshape.2106), calls=%async_computation | async-start | bytes 2703360 | tf_op jit(solution)/shard_map/all_to_all | solution.py:157
  220.2 6.3 %copy-start.10 = (pred[512]{0:T(512)(128)(4,1)S(1)}, pred[512]{0:T(512)(128)(4,1)}, u32[]{:S(2)}) copy-start(pred[512]{0:T(512)(128)(4,1)} %get-tuple-element.12) | copy-start | bytes 1540
  220.2 6.3 %copy-start.11 = (pred[512]{0:T(512)(128)(4,1)S(1)}, pred[512]{0:T(512)(128)(4,1)}, u32[]{:S(2)}) copy-start(pred[512]{0:T(512)(128)(4,1)} %get-tuple-element.13) | copy-start | bytes 1540
  220.3 6.3 %copy-start.12 = (pred[512]{0:T(512)(128)(4,1)S(1)}, pred[512]{0:T(512)(128)(4,1)}, u32[]{:S(2)}) copy-start(pred[512]{0:T(512)(128)(4,1)} %get-tuple-element.14) | copy-start | bytes 1540
  220.3 6.3 %copy-start.13 = (pred[512]{0:T(512)(128)(4,1)S(1)}, pred[512]{0:T(512)(128)(4,1)}, u32[]{:S(2)}) copy-start(pred[512]{0:T(512)(128)(4,1)} %get-tuple-element.15) | copy-start | bytes 1540
  220.3 6.3 %copy-start.14 = (pred[220]{0:T(512)(128)(4,1)S(1)}, pred[220]{0:T(512)(128)(4,1)}, u32[]{:S(2)}) copy-start(pred[220]{0:T(512)(128)(4,1)} %get-tuple-element.106) | copy-start | bytes 664
  220.3 6.3 %copy-start.15 = (pred[220]{0:T(512)(128)(4,1)S(1)}, pred[220]{0:T(512)(128)(4,1)}, u32[]{:S(2)}) copy-start(pred[220]{0:T(512)(128)(4,1)} %get-tuple-element.107) | copy-start | bytes 664
  220.3 6.3 %copy-start.16 = (pred[220]{0:T(512)(128)(4,1)S(1)}, pred[220]{0:T(512)(128)(4,1)}, u32[]{:S(2)}) copy-start(pred[220]{0:T(512)(128)(4,1)} %get-tuple-element.108) | copy-start | bytes 664
  230.9 16.8 %all-to-all-start.1 = ((f32[220,1,512]{2,1,0:T(1,128)}), f32[220,1,512]{2,1,0:T(1,128)S(1)}, u32[]{:S(2)}, u32[]{:S(2)}) async-start(f32[220,1,512]{2,1,0:T(1,128)} %copy.74), calls=%async_computation.1 | async-start | bytes 901120 | tf_op jit(solution)/shard_map/all_to_all | solution.py:177
  249.6 6.1 %copy-start = (f32[55,1,2047]{2,0,1:T(8,128)S(1)}, f32[55,1,2047]{2,0,1:T(8,128)}, u32[]{:S(2)}) copy-start(f32[55,1,2047]{2,0,1:T(8,128)} %get-tuple-element.30) | copy-start | bytes 1351024
  249.6 6.1 %copy-start.1 = (f32[55,1,2047]{2,0,1:T(8,128)S(1)}, f32[55,1,2047]{2,0,1:T(8,128)}, u32[]{:S(2)}) copy-start(f32[55,1,2047]{2,0,1:T(8,128)} %get-tuple-element.31) | copy-start | bytes 1351024
Sparse Core Ops, SparseCore 0:
  69.9 46.8 all-gather.2
where the time goes:
time: 266 us
  waiting for transfers between devices  141 us (53%)
  local copies, waits for them, and re-layouts  44.4 us (17%)
  starting transfers between devices  30.2 us (11%)
  other arithmetic  19.7 us (7%)
  matrix products  15.4 us (6%)
  between operations  14.5 us (5%)
    all_gather x1, waiting for transfers between devices, on_device(): lax.all_gather(flat_rough, 'modes', axis=0, tiled=True)  42.7 us
    ppermute x2, waiting for transfers between devices, padded_2(): lax.ppermute(lax.slice_in_dim(block, 0, width, axis=dim), axis, backward)  37.3 us
    all_to_all x1, waiting for transfers between devices, on_device(): lax.all_to_all(grads, 'modes', split_axis=3, concat_axis=1, tiled=True)  29.8 us
    ppermute x2, waiting for transfers between devices, padded_2(): lax.ppermute(lax.slice_in_dim(block, block.shape[dim] - width, None, axis...  19.9 us
    unnamed x39, local copies, waits for them, and re-layouts  17.5 us
    ppermute x2, starting transfers between devices, padded_2(): lax.ppermute(lax.slice_in_dim(block, block.shape[dim] - width, None, axis...  17.1 us
    all_to_all x1, waiting for transfers between devices, on_device(): lax.all_to_all(heat_points, 'modes', split_axis=0, concat_axis=2, tiled=T...  11.5 us
    all_to_all x3, local copies, waits for them, and re-layouts, on_device(): lax.all_to_all(grads, 'modes', split_axis=3, concat_axis=1, tiled=True)  6.9 us
  transfers between devices with their start and end apart: 7, of which 7 were waited for; matrix products, arithmetic and copies ran while one was open for 5% of the time, Pallas kernels for 0%

commit v1 on v0

--- a/solution.py
+++ b/solution.py
@@ -139,7 +139,9 @@
     mixed = jnp.einsum(
         "mij,jc->mic",
         row_coup,
-        lax.all_gather(flat_rough, "modes", axis=0, tiled=True),
+        jnp.concatenate(
+            lax.all_to_all(jnp.stack([flat_rough] * lax.axis_size("modes")), "modes", 0, 0), axis=0
+        ),
         precision=hp,
     )
     applied = jnp.sum(coeff_flat[:, None, :] * mixed, axis=0)

time: 266 us -> 238 us (0.89)
  the two profiles are of different devices: /device:TPU:59 before, /device:TPU:5 now
where the time goes in v1:
time: 238 us; the launch traced here: 237 us
  waiting for transfers between devices  120 us (50%)
  local copies, waits for them, and re-layouts  46.3 us (19%)
  starting transfers between devices  35.5 us (15%)
  other arithmetic  19.7 us (8%)
  matrix products  14.8 us (6%)
    ppermute x2, waiting for transfers between devices, padded_2(): lax.ppermute(lax.slice_in_dim(block, 0, width, axis=dim), axis, backward)  41.5 us
    all_to_all x1, waiting for transfers between devices, on_device(): lax.all_to_all(jnp.stack([flat_rough] * lax.axis_size('modes')), 'modes',...  31.3 us
    all_to_all x1, waiting for transfers between devices, on_device(): lax.all_to_all(grads, 'modes', split_axis=3, concat_axis=1, tiled=True)  28.5 us
    ppermute x2, starting transfers between devices, padded_2(): lax.ppermute(lax.slice_in_dim(block, block.shape[dim] - width, None, axis...  18.1 us
    unnamed x39, local copies, waits for them, and re-layouts  17.5 us
    all_to_all x1, waiting for transfers between devices, on_device(): lax.all_to_all(heat_points, 'modes', split_axis=0, concat_axis=2, tiled=T...  11.5 us
    ppermute x2, waiting for transfers between devices, padded_2(): lax.ppermute(lax.slice_in_dim(block, block.shape[dim] - width, None, axis...  7.18 us
    all_to_all x3, local copies, waits for them, and re-layouts, on_device(): lax.all_to_all(grads, 'modes', split_axis=3, concat_axis=1, tiled=True)  6.9 us
  transfers between devices with their start and end apart: 7, of which 6 were waited for; matrix products, arithmetic and copies ran while one was open for 6% of the time, Pallas kernels for 0%

profile of v1, /device:TPU:5, one launch (start us, length us, event | category | flops | bytes accessed | tf_op | source)
XLA Modules:
  0.0 237.4 jit_solution(10916193212295268948)
XLA Ops:
  2.9 2.6 %collective-permute-start.1 = (f32[2,55,1,2048]{3,0,2,1:T(2,128)S(1)}, f32[2,55,1,2048]{3,0,2,1:T(2,128)}, u32[]{:S(2)}, u32[]{:S(2)}) collective-permute-start(f32[2,55,1,2048]{3,0,2,1:T(2,128)S(1)} %copy.67), channel_id=1, source_target_pairs={{4,0},{8,4},{12,8},{16,12},{20,16},{24,20},{28,24},{32,28},{36,32}... | collective-permute-start | bytes 2703368 | tf_op jit(solution)/shard_map/ppermute | solution.py:25
  5.5 10.5 %collective-permute-start = (f32[2,55,1,2048]{3,0,2,1:T(2,128)S(1)}, f32[2,55,1,2048]{3,0,2,1:T(2,128)}, u32[]{:S(2)}, u32[]{:S(2)}) collective-permute-start(f32[2,55,1,2048]{3,0,2,1:T(2,128)S(1)} %copy.67), channel_id=1, source_target_pairs={{0,4},{4,8},{8,12},{12,16},{16,20},{20,24},{24,28},{28,32},{32,36}... | collective-permute-start | bytes 2703368 | tf_op jit(solution)/shard_map/ppermute | solution.py:22
  20.8 26.7 %collective-permute-done.1 = f32[2,55,1,2048]{3,0,2,1:T(2,128)} collective-permute-done((f32[2,55,1,2048]{3,0,2,1:T(2,128)S(1)}, f32[2,55,1,2048]{3,0,2,1:T(2,128)}, u32[]{:S(2)}, u32[]{:S(2)}) %collective-permute-start.1) | collective-permute-done | bytes 901152 | tf_op jit(solution)/shard_map/ppermute | solution.py:25
  49.2 7.2 %collective-permute-done = f32[2,55,1,2048]{3,0,2,1:T(2,128)} collective-permute-done((f32[2,55,1,2048]{3,0,2,1:T(2,128)S(1)}, f32[2,55,1,2048]{3,0,2,1:T(2,128)}, u32[]{:S(2)}, u32[]{:S(2)}) %collective-permute-start) | collective-permute-done | bytes 901152 | tf_op jit(solution)/shard_map/ppermute | solution.py:22
  61.0 4.4 %all-to-all-start = ((f32[4,55,2048]{2,1,0:T(8,128)}), f32[4,55,2048]{2,1,0:T(8,128)}, u32[]{:S(2)}, u32[]{:S(2)}) async-start(f32[4,55,2048]{2,1,0:T(8,128)} %stack.18), calls=%async_computation | async-start | bytes 3670016 | tf_op jit(solution)/shard_map/all_to_all | solution.py:143
  69.7 31.3 %all-to-all-done = f32[4,55,2048]{2,1,0:T(8,128)} async-done(((f32[4,55,2048]{2,1,0:T(8,128)}), f32[4,55,2048]{2,1,0:T(8,128)}, u32[]{:S(2)}, u32[]{:S(2)}) %all-to-all-start) | async-done | bytes 1802272 | tf_op jit(solution)/shard_map/all_to_all | solution.py:143
  102.7 5.3 %multiply_reduce_fusion = f32[55,2048]{1,0:T(8,128)S(1)} fusion(f32[10,55,220]{2,1,0:T(8,128)} %select_dynamic-update-slice_fusion, f32[220,2048,1]{1,0,2:T(8,128)S(1)} %reshape.2095, f32[10,2048]{1,0:T(8,128)S(1)} %multiply_bitcast_fusion.1), kind=kOutput, calls=%fused_computation | convolution fusion | flops 2975836160 | bytes 2818720 | tf_op jit(solution)/shard_map/mij,jc->mic/dot_general | solution.py:139
  110.9 7.5 %collective-permute-start.3 = (f32[55,1,2048]{2,0,1:T(8,128)S(1)}, f32[55,1,2048]{2,0,1:T(8,128)S(1)}, u32[]{:S(2)}, u32[]{:S(2)}) collective-permute-start(f32[55,1,2048]{2,0,1:T(8,128)S(1)} %fusion.39), channel_id=1, source_target_pairs={{0,4},{4,8},{8,12},{12,16},{16,20},{20,24},{24,28},{28,32},{32,36}... | collective-permute-start | bytes 1351688 | tf_op jit(solution)/shard_map/ppermute | solution.py:22
  118.8 14.8 %collective-permute-done.2 = f32[55,1,2048]{2,0,1:T(8,128)S(1)} collective-permute-done((f32[55,1,2048]{2,0,1:T(8,128)S(1)}, f32[55,1,2048]{2,0,1:T(8,128)S(1)}, u32[]{:S(2)}, u32[]{:S(2)}) %collective-permute-start.2) | collective-permute-done | bytes 450592 | tf_op jit(solution)/shard_map/ppermute | solution.py:25
  133.8 3.1 %copy.75 = f32[3,55,1,2048]{1,0,2,3:T(4,128)} copy(f32[3,55,1,2048]{3,1,2,0:T(8,128)S(1)} %pad_maximum_fusion.1) | data formatting | bytes 2703360 | tf_op jit(solution)/shard_map/stack | solution.py:55
  136.9 6.6 %reshape.2107 = f32[4,1,84480]{2,1,0:T(1,128)} reshape(f32[2048,1,3,55]{3,2,1,0:T(4,128)} %bitcast.196) | data formatting | bytes 2703360
  143.5 4.8 %all-to-all-start.1 = ((f32[4,1,84480]{2,1,0:T(1,128)}), f32[4,1,84480]{2,1,0:T(1,128)S(1)}, u32[]{:S(2)}, u32[]{:S(2)}) async-start(f32[4,1,84480]{2,1,0:T(1,128)} %reshape.2107), calls=%async_computation.1 | async-start | bytes 2703360 | tf_op jit(solution)/shard_map/all_to_all | solution.py:159
  149.7 28.5 %all-to-all-done.1 = f32[4,1,84480]{2,1,0:T(1,128)S(1)} async-done(((f32[4,1,84480]{2,1,0:T(1,128)}), f32[4,1,84480]{2,1,0:T(1,128)S(1)}, u32[]{:S(2)}, u32[]{:S(2)}) %all-to-all-start.1) | async-done | bytes 1351712 | tf_op jit(solution)/shard_map/all_to_all | solution.py:159
  178.8 5.7 %reduce.20 = f32[4,84480]{1,0:T(4,128)} reduce(f32[4,1,84480]{2,1,0:T(1,128)S(1)} %all-to-all-done.1, f32[]{:T(128)} %broadcast.1559), dimensions={1}, to_apply=%all_to_all.28.reduce_sub_computation | reduce | bytes 2703364 | tf_op jit(solution)/shard_map/all_to_all | solution.py:159
  184.4 6.9 %reshape.2108 = f32[2048,1,3,55]{3,2,1,0:T(4,128)} reshape(f32[4,84480]{1,0:T(4,128)} %reduce.20) | data formatting | bytes 2703360
  191.3 4.6 %copy.83 = f32[3,55,1,4,512]{4,3,1,0,2:T(4,128)} copy(f32[3,55,1,4,512]{1,0,4,3,2:T(4,128)} %bitcast.197) | data formatting | bytes 2703360 | tf_op jit(solution)/shard_map/all_to_all | solution.py:159
  199.0 6.3 %multiply_reduce_fusion.1 = f32[512,512]{1,0:T(8,128)S(1)} fusion(f32[3,220,512]{2,1,0:T(8,128)} %reshape.2094, f32[512]{0:T(512)S(1)} %bitcast.231, f32[512]{0:T(512)S(1)} %bitcast.279, f32[512]{0:T(512)S(1)} %bitcast.259, f32[220]{0:T(256)S(1)} %get-tuple-element.133, f32[512]{0:T(512)S(1)} %bitcast.233, f32[512]{0:T(512)S(1)} %bitcast.277, ...), kind=kOutput, calls=%fused_computation.1 | convolution fusion | flops 2084474880 | bytes 2469412 | tf_op jit(solution)/shard_map/qi,kixn->kqxn/dot_general | solution.py:156
  205.4 3.1 %convolution_bitcast_fusion = f32[220,1,512]{2,0,1:T(8,128)S(1)} fusion(f32[512,512]{1,0:T(8,128)S(1)} %multiply_reduce_fusion.1, f32[512]{0:T(512)S(1)} %bitcast.285, f32[512]{0:T(512)S(1)} %bitcast.286, f32[512]{0:T(512)S(1)} %bitcast.287, f32[512]{0:T(512)S(1)} %bitcast.284, f32[512]{0:T(512)S(1)} %bitcast.283, pred[512]{0:T(512)(128)(4,1)S(1)} %copy-done.13, ...), kind=kOutput, calls=%fused_computation.6 | convolution fusion | flops 701628416 | bytes 1582628 | tf_op jit(solution)/shard_map/iq,qxn->ixn/dot_general | solution.py:178
  209.7 3.7 %all-to-all-start.2 = ((f32[220,1,512]{2,1,0:T(1,128)}), f32[220,1,512]{2,1,0:T(1,128)S(1)}, u32[]{:S(2)}, u32[]{:S(2)}) async-start(f32[220,1,512]{2,1,0:T(1,128)} %copy.78), calls=%async_computation.2 | async-start | bytes 901120 | tf_op jit(solution)/shard_map/all_to_all | solution.py:179
  214.9 11.5 %all-to-all-done.2 = f32[220,1,512]{2,1,0:T(1,128)S(1)} async-done(((f32[220,1,512]{2,1,0:T(1,128)}), f32[220,1,512]{2,1,0:T(1,128)S(1)}, u32[]{:S(2)}, u32[]{:S(2)}) %all-to-all-start.2) | async-done | bytes 450592 | tf_op jit(solution)/shard_map/all_to_all | solution.py:179
  226.4 1.9 reduce.11
  228.3 1.9 all_to_all.32
  230.3 2.1 copy.79
  232.4 2.1 all_to_all.34
  (109 shorter events, 33.2 us)
Async XLA Ops:
  2.1 14.0 %copy-start.4 = (s32[220,9]{0,1:T(8,128)S(1)}, s32[220,9]{0,1:T(8,128)}, u32[]{:S(2)}) copy-start(s32[220,9]{0,1:T(8,128)} %param.15) | copy-start | bytes 23764
  2.2 14.9 %copy-start.7 = (s32[1,2048]{1,0:T(1,128)S(1)}, s32[1,2048]{1,0:T(1,128)}, u32[]{:S(2)}) copy-start(s32[1,2048]{1,0:T(1,128)} %param.13) | copy-start | bytes 24580
  2.2 15.7 %copy-start.5 = (f32[1,2048]{1,0:T(1,128)S(1)}, f32[1,2048]{1,0:T(1,128)}, u32[]{:S(2)}) copy-start(f32[1,2048]{1,0:T(1,128)} %param.12) | copy-start | bytes 24580
  2.2 15.6 %copy-start.8 = (s32[512]{0:T(512)S(1)}, s32[512]{0:T(512)}, u32[]{:S(2)}) copy-start(s32[512]{0:T(512)} %param.17) | copy-start | bytes 6148
  2.2 16.5 %copy-start.9 = (f32[4,9]{1,0:T(4,128)S(1)}, f32[4,9]{1,0:T(4,128)}, u32[]{:S(2)}) copy-start(f32[4,9]{1,0:T(4,128)} %param.14) | copy-start | bytes 436
  2.9 44.6 %collective-permute-start.1 = (f32[2,55,1,2048]{3,0,2,1:T(2,128)S(1)}, f32[2,55,1,2048]{3,0,2,1:T(2,128)}, u32[]{:S(2)}, u32[]{:S(2)}) collective-permute-start(f32[2,55,1,2048]{3,0,2,1:T(2,128)S(1)} %copy.67), channel_id=1, source_target_pairs={{4,0},{8,4},{12,8},{16,12},{20,16},{24,20},{28,24},{32,28},{36,32}... | collective-permute-start | bytes 2703368 | tf_op jit(solution)/shard_map/ppermute | solution.py:25
  5.5 50.9 %collective-permute-start = (f32[2,55,1,2048]{3,0,2,1:T(2,128)S(1)}, f32[2,55,1,2048]{3,0,2,1:T(2,128)}, u32[]{:S(2)}, u32[]{:S(2)}) collective-permute-start(f32[2,55,1,2048]{3,0,2,1:T(2,128)S(1)} %copy.67), channel_id=1, source_target_pairs={{0,4},{4,8},{8,12},{12,16},{16,20},{20,24},{24,28},{28,32},{32,36}... | collective-permute-start | bytes 2703368 | tf_op jit(solution)/shard_map/ppermute | solution.py:22
  61.0 39.9 %all-to-all-start = ((f32[4,55,2048]{2,1,0:T(8,128)}), f32[4,55,2048]{2,1,0:T(8,128)}, u32[]{:S(2)}, u32[]{:S(2)}) async-start(f32[4,55,2048]{2,1,0:T(8,128)} %stack.18), calls=%async_computation | async-start | bytes 3670016 | tf_op jit(solution)/shard_map/all_to_all | solution.py:143
  102.7 5.3 %copy-start.2 = (f32[55,1,2048]{2,1,0:T(1,128)S(1)}, f32[55,1,2048]{2,1,0:T(1,128)}, u32[]{:S(2)}) copy-start(f32[55,1,2048]{2,1,0:T(1,128)} %param.9) | copy-start | bytes 1351684
  102.7 5.3 %copy-start.3 = (f32[55,1,2048]{2,1,0:T(1,128)S(1)}, f32[55,1,2048]{2,1,0:T(1,128)}, u32[]{:S(2)}) copy-start(f32[55,1,2048]{2,1,0:T(1,128)} %param.10) | copy-start | bytes 1351684
  108.9 24.7 %collective-permute-start.2 = (f32[55,1,2048]{2,0,1:T(8,128)S(1)}, f32[55,1,2048]{2,0,1:T(8,128)S(1)}, u32[]{:S(2)}, u32[]{:S(2)}) collective-permute-start(f32[55,1,2048]{2,0,1:T(8,128)S(1)} %fusion.39), channel_id=1, source_target_pairs={{4,0},{8,4},{12,8},{16,12},{20,16},{24,20},{28,24},{32,28},{36,32}... | collective-permute-start | bytes 1351688 | tf_op jit(solution)/shard_map/ppermute | solution.py:25
  110.9 22.8 %collective-permute-start.3 = (f32[55,1,2048]{2,0,1:T(8,128)S(1)}, f32[55,1,2048]{2,0,1:T(8,128)S(1)}, u32[]{:S(2)}, u32[]{:S(2)}) collective-permute-start(f32[55,1,2048]{2,0,1:T(8,128)S(1)} %fusion.39), channel_id=1, source_target_pairs={{0,4},{4,8},{8,12},{12,16},{16,20},{20,24},{24,28},{28,32},{32,36}... | collective-permute-start | bytes 1351688 | tf_op jit(solution)/shard_map/ppermute | solution.py:22
  143.5 4.8 %copy-start.6 = (s32[512,9]{0,1:T(8,128)S(1)}, s32[512,9]{0,1:T(8,128)}, u32[]{:S(2)}) copy-start(s32[512,9]{0,1:T(8,128)} %param.16) | copy-start | bytes 55300
  143.5 34.7 %all-to-all-start.1 = ((f32[4,1,84480]{2,1,0:T(1,128)}), f32[4,1,84480]{2,1,0:T(1,128)S(1)}, u32[]{:S(2)}, u32[]{:S(2)}) async-start(f32[4,1,84480]{2,1,0:T(1,128)} %reshape.2107), calls=%async_computation.1 | async-start | bytes 2703360 | tf_op jit(solution)/shard_map/all_to_all | solution.py:159
  199.0 6.3 %copy-start.10 = (pred[512]{0:T(512)(128)(4,1)S(1)}, pred[512]{0:T(512)(128)(4,1)}, u32[]{:S(2)}) copy-start(pred[512]{0:T(512)(128)(4,1)} %get-tuple-element.12) | copy-start | bytes 1540
  199.0 6.3 %copy-start.11 = (pred[512]{0:T(512)(128)(4,1)S(1)}, pred[512]{0:T(512)(128)(4,1)}, u32[]{:S(2)}) copy-start(pred[512]{0:T(512)(128)(4,1)} %get-tuple-element.13) | copy-start | bytes 1540
  199.0 6.3 %copy-start.12 = (pred[512]{0:T(512)(128)(4,1)S(1)}, pred[512]{0:T(512)(128)(4,1)}, u32[]{:S(2)}) copy-start(pred[512]{0:T(512)(128)(4,1)} %get-tuple-element.14) | copy-start | bytes 1540
  199.0 6.3 %copy-start.13 = (pred[512]{0:T(512)(128)(4,1)S(1)}, pred[512]{0:T(512)(128)(4,1)}, u32[]{:S(2)}) copy-start(pred[512]{0:T(512)(128)(4,1)} %get-tuple-element.15) | copy-start | bytes 1540
  199.0 6.3 %copy-start.14 = (pred[220]{0:T(512)(128)(4,1)S(1)}, pred[220]{0:T(512)(128)(4,1)}, u32[]{:S(2)}) copy-start(pred[220]{0:T(512)(128)(4,1)} %get-tuple-element.106) | copy-start | bytes 664
  199.0 6.3 %copy-start.15 = (pred[220]{0:T(512)(128)(4,1)S(1)}, pred[220]{0:T(512)(128)(4,1)}, u32[]{:S(2)}) copy-start(pred[220]{0:T(512)(128)(4,1)} %get-tuple-element.107) | copy-start | bytes 664
  199.0 6.3 %copy-start.16 = (pred[220]{0:T(512)(128)(4,1)S(1)}, pred[220]{0:T(512)(128)(4,1)}, u32[]{:S(2)}) copy-start(pred[220]{0:T(512)(128)(4,1)} %get-tuple-element.108) | copy-start | bytes 664
  209.7 16.8 %all-to-all-start.2 = ((f32[220,1,512]{2,1,0:T(1,128)}), f32[220,1,512]{2,1,0:T(1,128)S(1)}, u32[]{:S(2)}, u32[]{:S(2)}) async-start(f32[220,1,512]{2,1,0:T(1,128)} %copy.78), calls=%async_computation.2 | async-start | bytes 901120 | tf_op jit(solution)/shard_map/all_to_all | solution.py:179
  228.3 6.1 %copy-start = (f32[55,1,2047]{2,0,1:T(8,128)S(1)}, f32[55,1,2047]{2,0,1:T(8,128)}, u32[]{:S(2)}) copy-start(f32[55,1,2047]{2,0,1:T(8,128)} %get-tuple-element.30) | copy-start | bytes 1351024
  228.3 6.1 %copy-start.1 = (f32[55,1,2047]{2,0,1:T(8,128)S(1)}, f32[55,1,2047]{2,0,1:T(8,128)}, u32[]{:S(2)}) copy-start(f32[55,1,2047]{2,0,1:T(8,128)} %get-tuple-element.31) | copy-start | bytes 1351024
